TPU v7x, 512 devices: a whole 4x8x8 slice. The times are simulated.
512 devices in a mesh: row: 16 (over z, core), col: 32 (over x, y).
Axes of the slice: x: 4, y: 8, z: 8, core: 2. Of those that a mesh axis runs over, the one named last changes fastest.
Arguments:
- strip: float32 [20480, 128], P('row'), may hold values from -6 to 6
- block_below: float32 [64, 64], replicated, may hold values from -1 to 1
- inverse_first: float32 [64, 64], replicated, may hold values from -0.5 to 1.5, as said below
- inverse_second: float32 [64, 64], replicated, may hold values from -0.5 to 1.5, as said below
- cotangent: float32 [20480, 20480], P('row', 'col'), may hold values from -0.0390625 to 0.0390625
Outputs:
- strip_grad: float32 [20480, 128], P('row')
Inputs may be any that keep to these rules, and one draw needn't show every extreme that they name: inverse_first is lower triangular with its diagonal in 0.5 to 1.5. inverse_second is lower triangular with its diagonal in 0.5 to 1.5.
All inputs are finite; a program needn't handle non-finite values.
Results may differ from a plain program's by a relative error of at most 0.00007.
Values sent between devices are 32-bit elements; how exact they have to be, the bound alone decides.
A program may use at most 64 MiB of HBM per device.

v0:
```python
import jax
import jax.numpy as jnp
from jax import lax
from jax.sharding import PartitionSpec as P


def from_root(value, axis, source):
    kept = jnp.where(lax.axis_index(axis) == source, value, 0).astype(value.dtype)
    return lax.psum(kept, axis)


def mul(left, right):
    return jnp.dot(left, right, precision=lax.Precision.HIGHEST, preferred_element_type=jnp.float32)


def finish(bar_sum, left_block, inverse_first, inverse_second, panel):
    bar_updated = mul(-bar_sum[:, panel:], inverse_second)
    bar_first = -bar_sum[:, :panel] - mul(bar_updated, left_block)
    return jnp.concatenate([mul(bar_first, inverse_first), bar_updated], axis=1)


def shards(strip, block_below, inverse_first, inverse_second, cotangent):
    panel = inverse_first.shape[0]
    cols_here = cotangent.shape[1]
    ratio = lax.axis_size("col") // lax.axis_size("row")
    col_id = lax.axis_index("col")
    owner = col_id // ratio
    offset = col_id % ratio * cols_here
    lower_first = mul(strip[:, :panel], inverse_first.T)
    left_block = mul(block_below, inverse_first.T)
    updated = strip[:, panel:] - mul(lower_first, left_block.T)
    col_first = from_root(lax.dynamic_slice_in_dim(lower_first, offset, cols_here, 0), "row", owner)
    lower_second = mul(updated, inverse_second.T)
    col_second = from_root(
        lax.dynamic_slice_in_dim(lower_second, offset, cols_here, 0), "row", owner
    )
    col_lower = jnp.concatenate([col_first, col_second], axis=1)
    lower = jnp.concatenate([lower_first, lower_second], axis=1)
    transposed = lax.dot_general(
        cotangent,
        lower,
        (((0,), (0,)), ((), ())),
        precision=lax.Precision.HIGHEST,
        preferred_element_type=jnp.float32,
    )
    col_total = lax.psum(transposed, "row")
    row_index = lax.axis_index("row")
    pieces = []
    for member in range(ratio):
        pieces.append(from_root(col_total, "col", row_index * ratio + member))
    routed = jnp.concatenate(pieces, axis=0)
    local_sum = mul(cotangent, col_lower)
    row_total = lax.psum(local_sum, "col")
    row_total = row_total + routed
    return finish(row_total, left_block, inverse_first, inverse_second, panel)


def solution(mesh):
    return jax.shard_map(
        shards,
        mesh=mesh,
        in_specs=(P("row", None), P(), P(), P(), P("row", "col")),
        out_specs=P("row", None),
        check_vma=False,
    )
```

profile of v0, /device:TPU:64, one launch (start us, length us, event | category | flops | bytes accessed | tf_op | source)
XLA Modules:
  0.0 320.7 jit_solution(9730919756724847951)
XLA Ops:
  6.5 0.0 copy-start
  6.5 0.0 all-reduce.7.cloned.1.call-start
  6.5 1.1 fusion.11
  7.7 2.7 fusion.3
  10.3 0.0 copy-start.1
  10.3 2.5 convolution_subtract_fusion
  12.8 1.6 fusion.12
  14.5 0.0 copy-done
  14.5 3.8 %convolution_bitcast_fusion.1 = f32[640,128]{0,1:T(8,128)} fusion(f32[1280,640]{1,0:T(8,128)S(1)} %copy-done, f32[1280,64]{0,1:T(8,128)S(1)} %fusion.12, f32[1280,64]{0,1:T(8,128)} %fusion.3), kind=kOutput, calls=%fused_computation.3 | convolution fusion | flops 1258455040 | bytes 4259840 | tf_op jit(solution)/shard_map/dot_general | solution.py:39
  18.3 0.0 copy-done.1
  18.3 0.7 dynamic-slice_select_fusion
  19.1 0.0 all-reduce.7.cloned.1.call-update
  19.1 0.0 all-reduce.5.cloned.1.call-start
  19.1 118.0 %all-reduce.7.cloned.1.call-done = (f32[640,64]{0,1:T(8,128)}, f32[640,64]{0,1:T(8,128)}, f32[640,128]{0,1:T(8,128)}) async-done(((f32[640,64]{0,1:T(8,128)}, f32[640,64]{0,1:T(8,128)}, f32[640,128]{0,1:T(8,128)}), (f32[640,64]{0,1:T(8,128)}, f32[640,64]{0,1:T(8,128)}, f32[640,128]{0,1:T(8,128)})) %all-reduce.7.cloned.1.call-update) | async-done | bytes 655376 | tf_op jit(solution)/shard_map/psum | solution.py:9
  137.2 0.0 copy-start.2
  137.2 0.0 copy-start.4
  137.2 5.3 %convolution_bitcast_fusion = f32[1280,128]{0,1:T(8,128)} fusion(f32[1280,640]{1,0:T(8,128)S(1)} %copy-done, f32[640,64]{0,1:T(8,128)} %get-tuple-element.8, f32[640,64]{0,1:T(8,128)} %get-tuple-element.9), kind=kOutput, calls=%fused_computation.1 | convolution fusion | flops 1258373120 | bytes 4259840 | tf_op jit(solution)/shard_map/dot_general | solution.py:13
  142.5 0.0 copy-start.3
  142.5 0.0 copy-done.2
  142.5 0.9 broadcast_select_fusion.1
  143.4 0.0 all-reduce.5.cloned.1.call-update
  143.4 164.6 %all-reduce.5.cloned.1.call-done = (f32[1280,128]{0,1:T(8,128)}, f32[640,128]{0,1:T(8,128)}, f32[640,128]{0,1:T(8,128)}) async-done(((f32[1280,128]{0,1:T(8,128)}, f32[640,128]{0,1:T(8,128)}, f32[640,128]{0,1:T(8,128)}), (f32[1280,128]{0,1:T(8,128)}, f32[640,128]{0,1:T(8,128)}, f32[640,128]{0,1:T(8,128)})) %all-reduce.5.cloned.1.call-update) | async-done | bytes 1310736 | tf_op jit(solution)/shard_map/psum | solution.py:53
  308.0 1.3 maximum_add_fusion
  309.3 0.0 copy-done.4
  309.4 0.5 fusion.5
  309.8 0.5 convolution_subtract_fusion.1
  310.3 0.0 copy-done.3
  310.3 0.5 fusion.13
  310.8 0.9 pad_maximum_fusion
  311.7 2.2 copy.6
Async XLA Ops:
  6.5 7.9 %copy-start = (f32[1280,640]{1,0:T(8,128)S(1)}, f32[1280,640]{1,0:T(8,128)}, u32[]{:S(2)}) copy-start(f32[1280,640]{1,0:T(8,128)} %param.9) | copy-start | bytes 9830404
  6.5 130.6 %all-reduce.7.cloned.1.call-start = ((), (), s32[]{:S(2)}) async-start(), calls=%async_computation.1 | async-start | bytes 1310720 | tf_op jit(solution)/shard_map/psum | solution.py:9
  10.3 8.0 %copy-start.1 = (f32[1280,64]{0,1:T(8,128)S(1)}, f32[1280,64]{0,1:T(8,128)}, u32[]{:S(2)}) copy-start(f32[1280,64]{0,1:T(8,128)} %fusion.3) | copy-start | bytes 983044
  19.1 288.9 %all-reduce.5.cloned.1.call-start = ((), (), s32[]{:S(2)}) async-start(), calls=%async_computation | async-start | bytes 2621440 | tf_op jit(solution)/shard_map/psum | solution.py:53
  137.2 5.3 %copy-start.2 = (f32[640,128]{0,1:T(8,128)S(1)}, f32[640,128]{0,1:T(8,128)}, u32[]{:S(2)}) copy-start(f32[640,128]{0,1:T(8,128)} %get-tuple-element.10) | copy-start | bytes 983044
  137.2 172.2 %copy-start.4 = (f32[64,64]{1,0:T(8,128)S(1)}, f32[64,64]{1,0:T(8,128)}, u32[]{:S(2)}) copy-start(f32[64,64]{1,0:T(8,128)} %param.8) | copy-start | bytes 49156
  142.5 167.8 %copy-start.3 = (f32[64,64]{1,0:T(8,128)S(1)}, f32[64,64]{1,0:T(8,128)}, u32[]{:S(2)}) copy-start(f32[64,64]{1,0:T(8,128)} %param.7) | copy-start | bytes 49156
Sparse Core Ops, SparseCore 0:
  19.2 117.9 all-reduce.6
  143.5 164.4 all-reduce.4
where the time goes:
time: 321 us
  waiting for transfers between devices  283 us (88%)
  matrix products  18.5 us (6%)
  between operations  13.5 us (4%)
  other arithmetic  3.85 us (1%)
    psum x1, waiting for transfers between devices, shards(): row_total = lax.psum(local_sum, 'col')  165 us
    psum x1, waiting for transfers between devices, from_root(): return lax.psum(kept, axis)  118 us
    dot_general x8, matrix products, mul(): jnp.dot(left, right, precision=lax.Precision.HIGHEST, preferred_element_t...  14.6 us
  transfers between devices with their start and end apart: 2, of which 2 were waited for; matrix products, arithmetic and copies ran while one was open for 0% of the time, Pallas kernels for 0%

commit v1 on v0

--- a/solution.py
+++ b/solution.py
@@ -2,6 +2,14 @@
 import jax.numpy as jnp
 from jax import lax
 from jax.sharding import PartitionSpec as P
+
+
+def sum_by_hops(block, name):
+    n_dev, result = (lax.axis_size(name), block)
+    for far in [1 << k for k in range(n_dev.bit_length() - 1)]:
+        pairs = [(i, i ^ far) for i in range(n_dev)]
+        result = result + lax.ppermute(result, name, pairs)
+    return result
 
 
 def from_root(value, axis, source):
@@ -50,7 +58,7 @@
         pieces.append(from_root(col_total, "col", row_index * ratio + member))
     routed = jnp.concatenate(pieces, axis=0)
     local_sum = mul(cotangent, col_lower)
-    row_total = lax.psum(local_sum, "col")
+    row_total = sum_by_hops(local_sum, "col")
     row_total = row_total + routed
     return finish(row_total, left_block, inverse_first, inverse_second, panel)
 

time: 321 us -> 411 us (1.28)
  waiting for transfers between devices: 283 us -> 345 us
  starting transfers between devices: 0.04 us -> 23.6 us
  other arithmetic: 3.85 us -> 8.34 us
    ppermute x0 -> x5, waiting for transfers between devices: none -> 85.3 us  [sum_by_hops(): result = result + lax.ppermute(result, name, pairs)]
    psum x1, waiting for transfers between devices: 165 us -> 118 us  [shards(): col_total = lax.psum(transposed, 'row')]
    ppermute x0 -> x5, starting transfers between devices: none -> 23.5 us  [sum_by_hops(): result = result + lax.ppermute(result, name, pairs)]
    psum x1, waiting for transfers between devices: 118 us -> 142 us  [from_root(): return lax.psum(kept, axis)]
  transfers between devices with their start and end apart: 2 -> 7, of which waited for: 2 -> 6; matrix products, arithmetic and copies ran while one was open for 0% -> 1% of each run, Pallas kernels for 0% -> 0%
where the time goes in v1:
time: 411 us; the launch traced here: 410 us
  waiting for transfers between devices  345 us (84%)
  starting transfers between devices  23.6 us (6%)
  matrix products  17.6 us (4%)
  between operations  13.5 us (3%)
  other arithmetic  8.34 us (2%)
    psum x1, waiting for transfers between devices, from_root(): return lax.psum(kept, axis)  142 us
    psum x1, waiting for transfers between devices, shards(): col_total = lax.psum(transposed, 'row')  118 us
    ppermute x5, waiting for transfers between devices, sum_by_hops(): result = result + lax.ppermute(result, name, pairs)  85.3 us
    ppermute x5, starting transfers between devices, sum_by_hops(): result = result + lax.ppermute(result, name, pairs)  23.5 us
    dot_general x8, matrix products, mul(): jnp.dot(left, right, precision=lax.Precision.HIGHEST, preferred_element_t...  13.7 us
  transfers between devices with their start and end apart: 7, of which 6 were waited for; matrix products, arithmetic and copies ran while one was open for 1% of the time, Pallas kernels for 0%

profile of v1, /device:TPU:64, one launch (start us, length us, event | category | flops | bytes accessed | tf_op | source)
XLA Modules:
  0.0 410.2 jit_solution(18251166452339789202)
XLA Ops:
  6.5 0.0 copy-start
  6.5 0.0 all-reduce.7.cloned.1.call-start
  6.5 1.1 fusion.14
  7.7 2.7 fusion.3
  10.3 0.0 copy-start.1
  10.3 2.5 convolution_subtract_fusion
  12.8 1.6 fusion.15
  14.5 0.0 copy-done
  14.5 3.8 convolution_bitcast_fusion.1
  18.3 0.0 copy-done.1
  18.3 0.7 dynamic-slice_select_fusion
  19.0 0.0 all-reduce.7.cloned.1.call-update
  19.0 0.0 all-reduce.5.cloned.1.call-start
  19.1 118.2 %all-reduce.7.cloned.1.call-done = (f32[640,128]{0,1:T(8,128)}, f32[640,64]{0,1:T(8,128)}, f32[640,64]{0,1:T(8,128)}) async-done(((f32[640,128]{0,1:T(8,128)}, f32[640,64]{0,1:T(8,128)}, f32[640,64]{0,1:T(8,128)}), (f32[640,128]{0,1:T(8,128)}, f32[640,64]{0,1:T(8,128)}, f32[640,64]{0,1:T(8,128)})) %all-reduce.7.cloned.1.call-update) | async-done | bytes 655376 | tf_op jit(solution)/shard_map/psum | solution.py:54
  137.3 4.4 %convolution_bitcast_fusion = f32[1280,128]{0,1:T(8,128)S(1)} fusion(f32[1280,640]{1,0:T(8,128)S(1)} %copy-done, f32[640,64]{0,1:T(8,128)} %get-tuple-element.8, f32[640,64]{0,1:T(8,128)} %get-tuple-element.9), kind=kOutput, calls=%fused_computation.1 | convolution fusion | flops 1258373120 | bytes 4259840 | tf_op jit(solution)/shard_map/dot_general | solution.py:21
  141.7 3.4 collective-permute-start
  145.1 15.3 %collective-permute-done = f32[1280,128]{0,1:T(8,128)S(1)} collective-permute-done((f32[1280,128]{0,1:T(8,128)S(1)}, f32[1280,128]{0,1:T(8,128)S(1)}, u32[]{:S(2)}, u32[]{:S(2)}) %collective-permute-start) | collective-permute-done | bytes 655392 | tf_op jit(solution)/shard_map/ppermute | solution.py:11
  160.4 0.1 add.42
  160.5 4.3 %collective-permute-start.1 = (f32[1280,128]{0,1:T(8,128)S(1)}, f32[1280,128]{0,1:T(8,128)S(1)}, u32[]{:S(2)}, u32[]{:S(2)}) collective-permute-start(f32[1280,128]{0,1:T(8,128)S(1)} %add.42), channel_id=1, source_target_pairs={{0,2},{1,3},{2,0},{3,1},{4,6},{5,7},{6,4},{7,5},{8,10},{9,11},{10,... | collective-permute-start | bytes 1966088 | tf_op jit(solution)/shard_map/ppermute | solution.py:11
  164.8 28.5 %collective-permute-done.1 = f32[1280,128]{0,1:T(8,128)S(1)} collective-permute-done((f32[1280,128]{0,1:T(8,128)S(1)}, f32[1280,128]{0,1:T(8,128)S(1)}, u32[]{:S(2)}, u32[]{:S(2)}) %collective-permute-start.1) | collective-permute-done | bytes 655392 | tf_op jit(solution)/shard_map/ppermute | solution.py:11
  193.3 0.1 add.43
  193.3 7.4 %collective-permute-start.2 = (f32[1280,128]{0,1:T(8,128)S(1)}, f32[1280,128]{0,1:T(8,128)S(1)}, u32[]{:S(2)}, u32[]{:S(2)}) collective-permute-start(f32[1280,128]{0,1:T(8,128)S(1)} %add.43), channel_id=1, source_target_pairs={{0,4},{1,5},{2,6},{3,7},{4,0},{5,1},{6,2},{7,3},{8,12},{9,13},{10,... | collective-permute-start | bytes 1966088 | tf_op jit(solution)/shard_map/ppermute | solution.py:11
  200.7 29.2 %collective-permute-done.2 = f32[1280,128]{0,1:T(8,128)S(1)} collective-permute-done((f32[1280,128]{0,1:T(8,128)S(1)}, f32[1280,128]{0,1:T(8,128)S(1)}, u32[]{:S(2)}, u32[]{:S(2)}) %collective-permute-start.2) | collective-permute-done | bytes 655392 | tf_op jit(solution)/shard_map/ppermute | solution.py:11
  229.9 0.9 add.44
  230.8 0.0 copy-start.3
  230.8 3.5 collective-permute-start.3
  234.3 1.9 broadcast_select_fusion.1
  236.2 0.0 copy-start.2
  236.2 0.0 all-reduce.5.cloned.1.call-update
  236.2 12.4 %collective-permute-done.3 = f32[1280,128]{0,1:T(8,128)} collective-permute-done((f32[1280,128]{0,1:T(8,128)}, f32[1280,128]{0,1:T(8,128)}, u32[]{:S(2)}, u32[]{:S(2)}) %collective-permute-start.3) | collective-permute-done | bytes 655392 | tf_op jit(solution)/shard_map/ppermute | solution.py:11
  248.6 2.2 add.45
  250.8 4.9 %collective-permute-start.4 = (f32[1280,128]{0,1:T(8,128)}, f32[1280,128]{0,1:T(8,128)}, u32[]{:S(2)}, u32[]{:S(2)}) collective-permute-start(f32[1280,128]{0,1:T(8,128)} %add.45), channel_id=1, source_target_pairs={{0,16},{1,17},{2,18},{3,19},{4,20},{5,21},{6,22},{7,23},{8,24},{9,... | collective-permute-start | bytes 1966088 | tf_op jit(solution)/shard_map/ppermute | solution.py:11
  255.8 141.5 %all-reduce.5.cloned.1.call-done = (f32[640,128]{0,1:T(8,128)}, f32[640,128]{0,1:T(8,128)}) async-done(((f32[640,128]{0,1:T(8,128)}, f32[640,128]{0,1:T(8,128)}), (f32[640,128]{0,1:T(8,128)}, f32[640,128]{0,1:T(8,128)})) %all-reduce.5.cloned.1.call-update) | async-done | bytes 655376 | tf_op jit(solution)/shard_map/psum | solution.py:17
  397.3 0.0 collective-permute-done.4
  397.3 1.6 maximum_add_fusion
  398.8 0.0 copy-done.3
  398.9 0.5 fusion.5
  399.3 0.5 fusion.16
  399.8 0.0 copy-done.2
  399.8 0.5 fusion.7
  400.3 0.9 pad_maximum_fusion
  401.2 2.2 copy.6
Async XLA Ops:
  6.5 7.9 %copy-start = (f32[1280,640]{1,0:T(8,128)S(1)}, f32[1280,640]{1,0:T(8,128)}, u32[]{:S(2)}) copy-start(f32[1280,640]{1,0:T(8,128)} %param.9) | copy-start | bytes 9830404
  6.5 130.8 %all-reduce.7.cloned.1.call-start = ((), (), s32[]{:S(2)}) async-start(), calls=%async_computation.1 | async-start | bytes 1310720 | tf_op jit(solution)/shard_map/psum | solution.py:54
  10.3 8.0 %copy-start.1 = (f32[1280,64]{0,1:T(8,128)S(1)}, f32[1280,64]{0,1:T(8,128)}, u32[]{:S(2)}) copy-start(f32[1280,64]{0,1:T(8,128)} %fusion.3) | copy-start | bytes 983044
  19.0 378.2 %all-reduce.5.cloned.1.call-start = ((), (), s32[]{:S(2)}) async-start(), calls=%async_computation | async-start | bytes 1310720 | tf_op jit(solution)/shard_map/psum | solution.py:17
  141.7 18.7 %collective-permute-start = (f32[1280,128]{0,1:T(8,128)S(1)}, f32[1280,128]{0,1:T(8,128)S(1)}, u32[]{:S(2)}, u32[]{:S(2)}) collective-permute-start(f32[1280,128]{0,1:T(8,128)S(1)} %convolution_bitcast_fusion), channel_id=1, source_target_pairs={{0,1},{1,0},{2,3},{3,2},{4,5},{5,4},{6,7},{7,6},{8,9},{9,8},{10,11... | collective-permute-start | bytes 1966088 | tf_op jit(solution)/shard_map/ppermute | solution.py:11
  160.5 32.8 %collective-permute-start.1 = (f32[1280,128]{0,1:T(8,128)S(1)}, f32[1280,128]{0,1:T(8,128)S(1)}, u32[]{:S(2)}, u32[]{:S(2)}) collective-permute-start(f32[1280,128]{0,1:T(8,128)S(1)} %add.42), channel_id=1, source_target_pairs={{0,2},{1,3},{2,0},{3,1},{4,6},{5,7},{6,4},{7,5},{8,10},{9,11},{10,... | collective-permute-start | bytes 1966088 | tf_op jit(solution)/shard_map/ppermute | solution.py:11
  193.3 36.5 %collective-permute-start.2 = (f32[1280,128]{0,1:T(8,128)S(1)}, f32[1280,128]{0,1:T(8,128)S(1)}, u32[]{:S(2)}, u32[]{:S(2)}) collective-permute-start(f32[1280,128]{0,1:T(8,128)S(1)} %add.43), channel_id=1, source_target_pairs={{0,4},{1,5},{2,6},{3,7},{4,0},{5,1},{6,2},{7,3},{8,12},{9,13},{10,... | collective-permute-start | bytes 1966088 | tf_op jit(solution)/shard_map/ppermute | solution.py:11
  230.8 168.1 %copy-start.3 = (f32[64,64]{1,0:T(8,128)S(1)}, f32[64,64]{1,0:T(8,128)}, u32[]{:S(2)}) copy-start(f32[64,64]{1,0:T(8,128)} %param.8) | copy-start | bytes 49156
  230.8 17.8 %collective-permute-start.3 = (f32[1280,128]{0,1:T(8,128)}, f32[1280,128]{0,1:T(8,128)}, u32[]{:S(2)}, u32[]{:S(2)}) collective-permute-start(f32[1280,128]{0,1:T(8,128)} %add.44), channel_id=1, source_target_pairs={{0,8},{1,9},{2,10},{3,11},{4,12},{5,13},{6,14},{7,15},{8,0},{9,1},... | collective-permute-start | bytes 1966088 | tf_op jit(solution)/shard_map/ppermute | solution.py:11
  236.2 163.6 %copy-start.2 = (f32[64,64]{1,0:T(8,128)S(1)}, f32[64,64]{1,0:T(8,128)}, u32[]{:S(2)}) copy-start(f32[64,64]{1,0:T(8,128)} %param.7) | copy-start | bytes 49156
  250.8 146.5 %collective-permute-start.4 = (f32[1280,128]{0,1:T(8,128)}, f32[1280,128]{0,1:T(8,128)}, u32[]{:S(2)}, u32[]{:S(2)}) collective-permute-start(f32[1280,128]{0,1:T(8,128)} %add.45), channel_id=1, source_target_pairs={{0,16},{1,17},{2,18},{3,19},{4,20},{5,21},{6,22},{7,23},{8,24},{9,... | collective-permute-start | bytes 1966088 | tf_op jit(solution)/shard_map/ppermute | solution.py:11
Sparse Core Ops, SparseCore 0:
  19.2 118.0 all-reduce.6
  236.4 160.8 all-reduce.4
